TPU v7x, 32 devices: a whole 2x2x4 slice. The times are simulated.
32 devices in a mesh: grp: 4 (over y, x), tile: 8 (over z, core).
Axes of the slice: x: 2, y: 2, z: 4, core: 2. Of those that a mesh axis runs over, the one named last changes fastest.
Arguments:
- flow_fields: float32 [5, 256, 16, 128], P(None, 'tile', 'grp'), may hold values from -6 to 6
- turbulent_diffusivity: float32 [256, 16, 128], P('tile', 'grp'), may hold values from 0.05 to 0.3
- holder_unit: int32 [4, 256, 1], P('grp', 'tile'), may hold values from 0 to 7, as said below
- spray_volume_position: int32 [8, 1024, 128], P('tile'), may hold values from 0 to 511
- patch_pick_unreduced: int32 [8, 1024], P('tile'), may hold values from 0 to 1048575
- droplet_motion: float32 [8, 1024, 3, 128], P('tile'), may hold values from -6 to 6
- droplet_warmth: float32 [8, 1024, 128], P('tile'), may hold values from -6 to 6
- droplet_weightiness: float32 [8, 1024, 128], P('tile'), may hold values from 0.25 to 2
- droplet_multiplicity: float32 [8, 1024, 128], P('tile'), may hold values from 0.5 to 2
- living_spray_batches: int32 [8], P('tile'), may hold values from 1 to 1024, 4096 in all
Outputs:
- gas_next: float32 [5, 256, 16, 128], P(None, 'tile', 'grp')
Inputs may be any that keep to these rules, and one draw needn't show every extreme that they name: `holder_unit`: among the 32 tiles of one gas device (aligned blocks of 32 rows of owner, in order of its first two dimensions) no parcel device owns more than 8, and in every such block one parcel device owns exactly 8. Two parcel devices own no tile at all. Rows with g = 3 are not used. `living_spray_batches`: live blocks of a device are its first ones; the busiest parcel device has exactly 1024, and they sum to 4096.
All inputs are finite; a program needn't handle non-finite values.
Results may differ from a plain program's by a relative error of at most 0.0045.
Values may be sent and summed in bfloat16 or wider, within the bound.
A program may use at most 64 MiB of HBM per device.

v0:
```python
import jax
import jax.numpy as jnp
from jax import lax
from jax.sharding import PartitionSpec as P

BLOCK_GROUP = 64


def padded_2(block, sides, width):
    for axis, dim in sides:
        count = lax.axis_size(axis)
        forward = [(i, i + 1) for i in range(count - 1)]
        backward = [(target, source) for source, target in forward]
        low = lax.ppermute(
            lax.slice_in_dim(block, block.shape[dim] - width, None, axis=dim), axis, forward
        )
        high = lax.ppermute(lax.slice_in_dim(block, 0, width, axis=dim), axis, backward)
        block = jnp.concatenate([low, block, high], axis=dim)
    return block


def droplet_coupling_feeds(
    reached_markers, droplet_motion, droplet_warmth, droplet_weightiness, droplet_multiplicity
):
    gas_velocity = reached_markers[..., 0:3, :]
    fluid_warming_share = reached_markers[..., 3, :]
    gas_fuel = reached_markers[..., 4, :]
    relative = gas_velocity - droplet_motion
    speed_sq = jnp.sum(relative * relative, axis=-2)
    surface = droplet_weightiness ** (2.0 / 3.0)
    inverse_tau = 0.8 * (1.0 + 0.15 * (1.0 + speed_sq) ** 0.3435) / surface
    relaxation = 1.0 - jnp.exp(-0.5 * inverse_tau)
    new_velocity = droplet_motion + relaxation[..., None, :] * relative
    heating = 1.0 / (1.0 + jnp.exp(-(fluid_warming_share - gas_fuel)))
    leftover_liquid_load = jnp.exp(-0.3 * heating / surface)
    updated_droplet_load = droplet_weightiness * leftover_liquid_load
    warming_speed = 1.0 - jnp.exp(-0.25 * inverse_tau)
    updated_droplet_warmth = (
        droplet_warmth
        + warming_speed * (fluid_warming_share - droplet_warmth)
        - 0.5 * (1.0 - leftover_liquid_load)
    )
    momentum = (
        droplet_weightiness[..., None, :] * droplet_motion
        - updated_droplet_load[..., None, :] * new_velocity
    )
    enthalpy_content = (
        droplet_weightiness * droplet_warmth - updated_droplet_load * updated_droplet_warmth
    )
    stacked = jnp.concatenate(
        [
            momentum,
            enthalpy_content[..., None, :],
            (droplet_weightiness - updated_droplet_load)[..., None, :],
        ],
        axis=-2,
    )
    return droplet_multiplicity[..., None, :] * stacked


def local(
    flow_fields,
    turbulent_diffusivity,
    holder_unit,
    spray_volume_position,
    patch_pick_unreduced,
    droplet_motion,
    droplet_warmth,
    droplet_weightiness,
    droplet_multiplicity,
    living_spray_batches,
):
    group_count = lax.axis_size("grp")
    owners = lax.axis_size("tile")
    group_index = lax.axis_index("grp")
    gas_side = (group_index < group_count - 1).astype(jnp.float32)
    gas_field = flow_fields * gas_side
    nfield, planes, rows_y, z_cells = gas_field.shape
    tile_cells = rows_y * z_cells
    slot_depth = max(2, 2 * planes // owners)
    padded = padded_2(gas_field.astype(jnp.bfloat16), (("grp", 2), ("tile", 1)), 1).astype(
        gas_field.dtype
    )
    z_padded = jnp.pad(gas_field, ((0, 0), (0, 0), (0, 0), (1, 1)))
    beside = padded[:, 2:, 1:-1, :] + padded[:, :-2, 1:-1, :]
    beside = beside + padded[:, 1:-1, 2:, :] + padded[:, 1:-1, :-2, :]
    beside = beside + z_padded[:, :, :, 2:] + z_padded[:, :, :, :-2]
    laplace = beside - 6.0 * gas_field
    plane_owner = holder_unit[0, :, 0]
    positions = jnp.arange(planes, dtype=jnp.int32)
    same_owner = plane_owner[:, None] == plane_owner[None, :]
    plane_rank = jnp.sum(
        (same_owner & (positions[None, :] < positions[:, None])).astype(jnp.int32), axis=1
    )
    targets = jnp.arange(owners * slot_depth, dtype=jnp.int32)
    selector = (
        (plane_owner[None, :] == targets[:, None] // slot_depth)
        & (plane_rank[None, :] == targets[:, None] % slot_depth)
    ).astype(jnp.float32) * gas_side
    tile_rows = (
        gas_field.astype(jnp.bfloat16).transpose(1, 0, 2, 3).reshape(planes, nfield * tile_cells)
    )
    packed = jnp.dot(selector.astype(jnp.bfloat16), tile_rows, preferred_element_type=jnp.float32)
    packed = packed.astype(jnp.bfloat16).reshape(owners, slot_depth, nfield, tile_cells)
    slot_flags = jnp.sum(selector, axis=1).astype(jnp.int32).reshape(owners, slot_depth)
    lifted_tiles, lifted_flags = (
        lax.all_gather(packed[None], "grp", axis=0, tiled=True),
        lax.all_gather(slot_flags[None], "grp", axis=0, tiled=True),
    )
    arrived, arrived_flags = (
        lax.all_to_all(lifted_tiles, "tile", split_axis=1, concat_axis=1, tiled=True),
        lax.all_to_all(lifted_flags, "tile", split_axis=1, concat_axis=1, tiled=True),
    )
    gas_groups = group_count - 1
    slot_count = gas_groups * owners * slot_depth
    tile_table = arrived[:gas_groups].reshape(slot_count, nfield, tile_cells)
    valid = arrived_flags[:gas_groups].reshape(slot_count)
    owned_count = jnp.sum(valid)
    running = jnp.cumsum(valid)
    picked = patch_pick_unreduced[0] % jnp.maximum(owned_count, 1)
    matches = (valid[None, :] == 1) & (running[None, :] - 1 == picked[:, None])
    block_slot = jnp.sum(
        jnp.where(matches, jnp.arange(slot_count, dtype=jnp.int32)[None, :], 0), axis=1
    )
    live_count = living_spray_batches[0]
    share_size = (
        (live_count + group_count * BLOCK_GROUP - 1) // (group_count * BLOCK_GROUP) * BLOCK_GROUP
    )
    first_block = jnp.minimum(group_index * share_size, live_count)
    end_block = jnp.minimum(first_block + share_size, live_count)
    end_block = jnp.where(owned_count > 0, end_block, first_block)
    group_turns = (end_block - first_block + BLOCK_GROUP - 1) // BLOCK_GROUP
    parcel_cells = spray_volume_position[0]
    parcel_velocity = droplet_motion[0]
    droplet_warming_share = droplet_warmth[0]
    parcel_mass = droplet_weightiness[0]
    parcel_weight = droplet_multiplicity[0]
    cell_ids = jnp.arange(tile_cells, dtype=jnp.int32)

    def advance(step_index, totals):
        start = first_block + step_index * BLOCK_GROUP

        def block_slice(array):
            return lax.dynamic_slice_in_dim(array, start, BLOCK_GROUP, 0)

        block_ids = start + jnp.arange(BLOCK_GROUP, dtype=jnp.int32)
        keep_mask = (block_ids < end_block).astype(jnp.float32)
        slots_here = block_slice(block_slot)
        cells_here = block_slice(parcel_cells)
        tile_values = tile_table[slots_here]
        one_hot = (cells_here[:, :, None] == cell_ids[None, None, :]).astype(jnp.bfloat16)
        reached_markers = jnp.einsum(
            "bfc,bpc->bfp", tile_values, one_hot, preferred_element_type=jnp.float32
        )
        coupling_feeds = droplet_coupling_feeds(
            reached_markers,
            block_slice(parcel_velocity),
            block_slice(droplet_warming_share),
            block_slice(parcel_mass),
            block_slice(parcel_weight),
        )
        coupling_feeds = coupling_feeds * keep_mask[:, None, None]
        upper = coupling_feeds.astype(jnp.bfloat16)
        leftover = coupling_feeds - upper.astype(jnp.float32)
        middle = leftover.astype(jnp.bfloat16)
        lower = (leftover - middle.astype(jnp.float32)).astype(jnp.bfloat16)
        pieces = jnp.concatenate([upper, middle, lower], axis=1)
        deposited = jnp.einsum("bfp,bpc->bfc", pieces, one_hot, preferred_element_type=jnp.float32)
        per_block = (
            deposited[:, :nfield] + deposited[:, nfield : 2 * nfield] + deposited[:, 2 * nfield :]
        )
        return totals.at[slots_here].add(per_block)

    deposit = lax.fori_loop(
        0, group_turns, advance, jnp.zeros((slot_count, nfield, tile_cells), jnp.float32)
    )
    zero_block = jnp.zeros((1, owners, slot_depth, nfield, tile_cells), jnp.float32)
    outgoing = jnp.concatenate(
        [deposit.reshape(gas_groups, owners, slot_depth, nfield, tile_cells), zero_block], axis=0
    )
    spread = lax.all_to_all(outgoing, "tile", split_axis=1, concat_axis=1, tiled=True)
    landed = lax.psum_scatter(spread, "grp", scatter_dimension=0, tiled=True)
    incoming = landed.reshape(owners * slot_depth, nfield * tile_cells)
    placed = jnp.dot(
        selector.T, incoming, precision=lax.Precision.HIGHEST, preferred_element_type=jnp.float32
    )
    placed = placed.reshape(planes, nfield, rows_y, z_cells).transpose(1, 0, 2, 3)
    return (gas_field + 0.5 * turbulent_diffusivity * laplace + placed) * gas_side


def solution(mesh):
    in_specs = (
        P(None, "tile", "grp", None),
        P("tile", "grp", None),
        P("grp", "tile", None),
        P("tile", None, None),
        P("tile", None),
        P("tile", None, None, None),
        P("tile", None, None),
        P("tile", None, None),
        P("tile", None, None),
        P("tile"),
    )
    out_specs = P(None, "tile", "grp", None)
    return jax.shard_map(local, mesh=mesh, in_specs=in_specs, out_specs=out_specs, check_vma=False)
```

profile of v0, /device:TPU:0, one launch (start us, length us, event | category | flops | bytes accessed | tf_op | source)
XLA Modules:
  0.0 326.9 jit_solution(9831295287302092745)
XLA Ops:
  6.5 0.9 convert_reduce_fusion
  7.5 1.0 fusion.40
  8.5 0.1 copy.82
  8.7 1.7 convolution_convert_fusion
  10.4 0.7 select_reduce_fusion.1
  11.2 9.7 %all_gather.6 = s32[4,8,8]{2,1,0:T(8,128)S(1)} all-gather(s32[1,8,8]{2,1,0:T(8,128)S(1)} %convert_element_type.87), channel_id=1, replica_groups=mesh['grp'=4,'tile'=8] {'grp'}, dimensions={0}, use_global_device_ids=true | all-gather | bytes 1280 | tf_op jit(solution)/shard_map/all_gather | solution.py:108
  20.9 0.6 copy.79
  21.5 4.9 %all-to-all-start = ((s32[4,8,8]{2,0,1:T(4,128)}), s32[4,8,8]{2,0,1:T(4,128)S(1)}, u32[]{:S(2)}, u32[]{:S(2)}) async-start(s32[4,8,8]{2,0,1:T(4,128)} %copy.79), calls=%async_computation | async-start | bytes 32768 | tf_op jit(solution)/shard_map/all_to_all | solution.py:112
  26.4 15.6 %all-gather.2.cloned.1.call-done = bf16[4,8,8,5,512]{4,2,3,1,0:T(8,128)(2,1)} async-done(((bf16[1,8,8,5,512]{4,2,3,1,0:T(8,128)(2,1)}), bf16[4,8,8,5,512]{4,2,3,1,0:T(8,128)(2,1)}) %all-gather.2.cloned.1.call-update) | async-done | bytes 1310736 | tf_op jit(solution)/shard_map/all_gather | solution.py:107
  41.9 2.5 copy.83
  44.5 4.7 %all-to-all-start.1 = ((bf16[4,8,8,5,512]{4,2,3,0,1:T(8,128)(2,1)}), bf16[4,8,8,5,512]{4,2,3,0,1:T(8,128)(2,1)S(1)}, u32[]{:S(2)}, u32[]{:S(2)}) async-start(bf16[4,8,8,5,512]{4,2,3,0,1:T(8,128)(2,1)} %copy.83), calls=%async_computation.1 | async-start | bytes 2621440 | tf_op jit(solution)/shard_map/all_to_all | solution.py:111
  49.9 2.5 copy.105
  52.4 0.7 fusion.43
  54.4 0.1 broadcast_in_dim_reshape.7
  54.5 0.3 reduce-window.9
  54.9 0.1 slice_reduce_fusion
  55.1 0.4 broadcast_remainder_fusion
  55.5 0.2 select_reduce_fusion
  55.7 25.7 %all-to-all-done.1 = bf16[4,8,8,5,512]{4,2,3,0,1:T(8,128)(2,1)S(1)} async-done(((bf16[4,8,8,5,512]{4,2,3,0,1:T(8,128)(2,1)}), bf16[4,8,8,5,512]{4,2,3,0,1:T(8,128)(2,1)S(1)}, u32[]{:S(2)}, u32[]{:S(2)}) %all-to-all-start.1) | async-done | bytes 1310752 | tf_op jit(solution)/shard_map/all_to_all | solution.py:111
  81.4 0.1 slice.124
  81.5 0.1 copy.97
  81.6 0.6 copy.85
  82.2 2.1 broadcast_in_dim.54
  84.2 44.5 %while.14 = (s32[]{:T(128)}, f32[192,5,512]{2,1,0:T(8,128)}, s32[]{:T(128)}, s32[]{:T(128)}, s32[1024]{0:T(1024)S(1)}, /*index=5*/f32[1024,128]{1,0:T(8,128)}, f...) while((s32[]{:T(128)}, f32[192,5,512]{2,1,0:T(8,128)}, ...), condition=%wide.region_9.10_spmd.clone, body=%wide.region_6.9_spmd.clone.sunk | while | flops 178324864 | bytes 9770991 | solution.py:174
  84.3 0.6 gather_fusion
  84.9 0.8 constant_dynamic-slice_fusion.6
  85.7 4.3 %fusion.55 = f32[64,5,128]{2,1,0:T(8,128)S(1)} fusion(bf16[64,5,512]{2,1,0:T(8,128)(2,1)S(1)} %gather_fusion, s32[64,128]{1,0:T(8,128)S(1)} %constant_dynamic-slice_fusion.6), kind=kOutput, calls=%fused_computation.5.clone.1 | convolution fusion | flops 46137344 | bytes 524288 | tf_op jit(solution)/shard_map/while/body/bfc,bpc->bfp/dot_general | solution.py:152
  90.1 0.8 fusion.57
  91.0 1.0 multiply_reduce_fusion.2
  92.0 0.9 multiply_subtract_fusion.4
  92.9 1.0 multiply_subtract_fusion.5
  93.9 0.2 fusion.58
  94.1 4.1 %fusion.59 = f32[64,15,512]{2,1,0:T(8,128)S(1)} fusion(s32[64,128]{1,0:T(8,128)S(1)} %constant_dynamic-slice_fusion.6, bf16[64,5,128]{2,1,0:T(8,128)(2,1)S(1)} %get-tuple-element.392, bf16[64,5,128]{2,1,0:T(8,128)(2,1)S(1)} %get-tuple-element.393, bf16[64,5,128]{2,1,0:T(8,128)(2,1)S(1)} %get-tuple-element.394), kind=kOutput, calls=%fused_computation.4.clone.1 | convolution fusion | flops 130760704 | bytes 2244608 | tf_op jit(solution)/shard_map/while/body/bfp,bpc->bfc/dot_general | solution.py:168
  98.1 0.3 slice_add_fusion.7
  98.4 8.1 %scatter_fusion = f32[192,5,512]{2,1,0:T(8,128)} fusion(f32[192,5,512]{2,1,0:T(8,128)} %get-tuple-element.412, s32[64]{0:T(128)S(1)} %compare_select_fusion.2, f32[64,5,512]{2,1,0:T(8,128)S(1)} %slice_add_fusion.7), kind=kCustom, calls=%fused_computation.1.clone.clone.1 | custom fusion | flops 163840 | bytes 1966336 | tf_op jit(solution)/shard_map/while/body/scatter-add | solution.py:172
  106.5 0.6 gather_fusion
  107.1 0.8 constant_dynamic-slice_fusion.6
  107.9 4.3 %fusion.55 = f32[64,5,128]{2,1,0:T(8,128)S(1)} fusion(bf16[64,5,512]{2,1,0:T(8,128)(2,1)S(1)} %gather_fusion, s32[64,128]{1,0:T(8,128)S(1)} %constant_dynamic-slice_fusion.6), kind=kOutput, calls=%fused_computation.5.clone.1 | convolution fusion | flops 46137344 | bytes 524288 | tf_op jit(solution)/shard_map/while/body/bfc,bpc->bfp/dot_general | solution.py:152
  112.3 0.8 fusion.57
  113.2 1.0 multiply_reduce_fusion.2
  114.2 0.9 multiply_subtract_fusion.4
  115.1 1.0 multiply_subtract_fusion.5
  116.1 0.2 fusion.58
  116.3 4.1 %fusion.59 = f32[64,15,512]{2,1,0:T(8,128)S(1)} fusion(s32[64,128]{1,0:T(8,128)S(1)} %constant_dynamic-slice_fusion.6, bf16[64,5,128]{2,1,0:T(8,128)(2,1)S(1)} %get-tuple-element.392, bf16[64,5,128]{2,1,0:T(8,128)(2,1)S(1)} %get-tuple-element.393, bf16[64,5,128]{2,1,0:T(8,128)(2,1)S(1)} %get-tuple-element.394), kind=kOutput, calls=%fused_computation.4.clone.1 | convolution fusion | flops 130760704 | bytes 2244608 | tf_op jit(solution)/shard_map/while/body/bfp,bpc->bfc/dot_general | solution.py:168
  120.4 0.3 slice_add_fusion.7
  120.6 8.1 %scatter_fusion = f32[192,5,512]{2,1,0:T(8,128)} fusion(f32[192,5,512]{2,1,0:T(8,128)} %get-tuple-element.412, s32[64]{0:T(128)S(1)} %compare_select_fusion.2, f32[64,5,512]{2,1,0:T(8,128)S(1)} %slice_add_fusion.7), kind=kCustom, calls=%fused_computation.1.clone.clone.1 | custom fusion | flops 163840 | bytes 1966336 | tf_op jit(solution)/shard_map/while/body/scatter-add | solution.py:172
  128.7 3.0 copy.98
  131.7 0.3 concatenate.25.clone
  132.1 105.3 %all_to_all.15 = f32[4,8,8,5,512]{4,2,0,3,1:T(8,128)S(1)} all-to-all(f32[4,8,8,5,512]{4,2,0,3,1:T(8,128)S(1)} %concatenate.25.clone), channel_id=1, replica_groups=mesh['grp'=4,'tile'=8] {'tile'}, dimensions={1} | all-to-all | bytes 5242880 | tf_op jit(solution)/shard_map/all_to_all | solution.py:181
  237.4 1.8 copy.88
  239.2 3.4 %collective-permute-start = (bf16[5,32,1,128]{3,1,2,0:T(8,128)(2,1)S(1)}, bf16[5,32,1,128]{3,1,2,0:T(8,128)(2,1)S(1)}, u32[]{:S(2)}, u32[]{:S(2)}) collective-permute-start(bf16[5,32,1,128]{3,1,2,0:T(8,128)(2,1)S(1)} %get-tuple-element.293), channel_id=1, source_target_pairs={{0,8},{8,16},{16,24},{1,9},{9,17},{17,25},{2,10},{10,18},{18,26},{... | collective-permute-start | bytes 122888 | tf_op jit(solution)/shard_map/ppermute | solution.py:14
  242.7 1.3 collective-permute-start.1
  244.0 1.0 collective-permute-done
  245.0 4.6 %collective-permute-done.1 = bf16[5,32,1,128]{3,1,2,0:T(8,128)(2,1)S(1)} collective-permute-done((bf16[5,32,1,128]{3,1,2,0:T(8,128)(2,1)S(1)}, bf16[5,32,1,128]{3,1,2,0:T(8,128)(2,1)S(1)}, u32[]{:S(2)}, u32[]{:S(2)}) %collective-permute-start.1) | collective-permute-done | bytes 40992 | tf_op jit(solution)/shard_map/ppermute | solution.py:17
  249.6 1.3 collective-permute-start.2
  250.9 1.3 collective-permute-start.3
  252.3 0.6 dynamic-slice
  252.9 1.1 collective-permute-done.3
  254.0 0.1 maximum_convert_fusion
  254.1 62.3 %all-reduce.6.cloned.1.call-done = f32[4,8,8,5,512]{4,2,1,0,3:T(8,128)} async-done(((f32[4,8,8,5,512]{4,2,1,0,3:T(8,128)}), f32[4,8,8,5,512]{4,2,1,0,3:T(8,128)}) %all-reduce.6.cloned.1.call-update) | async-done | bytes 2621456
  316.5 1.8 constant_dynamic-slice_fusion.3
  318.3 0.2 dot_general.26
  318.6 0.6 fusion.18
  319.2 0.9 copy.91
  (41 shorter events, 0.9 us)
Async XLA Ops:
  6.5 35.4 %all-gather.2.cloned.1.call-start = ((), (), s32[]{:S(2)}) async-start(), calls=%async_computation.3 | async-start | bytes 1638400 | tf_op jit(solution)/shard_map/all_gather | solution.py:107
  21.5 23.0 %all-to-all-start = ((s32[4,8,8]{2,0,1:T(4,128)}), s32[4,8,8]{2,0,1:T(4,128)S(1)}, u32[]{:S(2)}, u32[]{:S(2)}) async-start(s32[4,8,8]{2,0,1:T(4,128)} %copy.79), calls=%async_computation | async-start | bytes 32768 | tf_op jit(solution)/shard_map/all_to_all | solution.py:112
  26.4 23.5 %copy-start = (f32[1,1024,3,128]{3,1,2,0:T(8,128)S(1)}, f32[1,1024,3,128]{3,1,2,0:T(8,128)}, u32[]{:S(2)}) copy-start(f32[1,1024,3,128]{3,1,2,0:T(8,128)} %param.17) | copy-start | bytes 4718596
  44.5 10.6 %copy-start.2 = (s32[1,1024]{1,0:T(1,128)S(1)}, s32[1,1024]{1,0:T(1,128)}, u32[]{:S(2)}) copy-start(s32[1,1024]{1,0:T(1,128)} %param.16) | copy-start | bytes 12292
  44.5 36.9 %all-to-all-start.1 = ((bf16[4,8,8,5,512]{4,2,3,0,1:T(8,128)(2,1)}), bf16[4,8,8,5,512]{4,2,3,0,1:T(8,128)(2,1)S(1)}, u32[]{:S(2)}, u32[]{:S(2)}) async-start(bf16[4,8,8,5,512]{4,2,3,0,1:T(8,128)(2,1)} %copy.83), calls=%async_computation.1 | async-start | bytes 2621440 | tf_op jit(solution)/shard_map/all_to_all | solution.py:111
  49.2 267.3 %all-reduce.6.cloned.1.call-start = ((), (), s32[]{:S(2)}) async-start(), calls=%async_computation.4 | async-start | bytes 5242880
  239.2 13.0 %copy-start.1 = (f32[32,4,128]{2,1,0:T(4,128)S(1)}, f32[32,4,128]{2,1,0:T(4,128)}, u32[]{:S(2)}) copy-start(f32[32,4,128]{2,1,0:T(4,128)} %param.13) | copy-start | bytes 196612
  239.2 13.1 %copy-start.4 = (u32[32]{0:T(128)S(1)}, u32[32]{0:T(128)}, u32[]{:S(2)}) copy-start(u32[32]{0:T(128)} %constant.197) | copy-start | bytes 388
  239.2 5.7 %collective-permute-start = (bf16[5,32,1,128]{3,1,2,0:T(8,128)(2,1)S(1)}, bf16[5,32,1,128]{3,1,2,0:T(8,128)(2,1)S(1)}, u32[]{:S(2)}, u32[]{:S(2)}) collective-permute-start(bf16[5,32,1,128]{3,1,2,0:T(8,128)(2,1)S(1)} %get-tuple-element.293), channel_id=1, source_target_pairs={{0,8},{8,16},{16,24},{1,9},{9,17},{17,25},{2,10},{10,18},{18,26},{... | collective-permute-start | bytes 122888 | tf_op jit(solution)/shard_map/ppermute | solution.py:14
  242.7 6.9 %collective-permute-start.1 = (bf16[5,32,1,128]{3,1,2,0:T(8,128)(2,1)S(1)}, bf16[5,32,1,128]{3,1,2,0:T(8,128)(2,1)S(1)}, u32[]{:S(2)}, u32[]{:S(2)}) collective-permute-start(bf16[5,32,1,128]{3,1,2,0:T(8,128)(2,1)S(1)} %get-tuple-element.294), channel_id=1, source_target_pairs={{8,0},{16,8},{24,16},{9,1},{17,9},{25,17},{10,2},{18,10},{26,18},{... | collective-permute-start | bytes 122888 | tf_op jit(solution)/shard_map/ppermute | solution.py:17
  249.6 69.0 %copy-start.3 = (s32[1,32,1]{1,2,0:T(1,128)S(1)}, s32[1,32,1]{1,2,0:T(1,128)}, u32[]{:S(2)}) copy-start(s32[1,32,1]{1,2,0:T(1,128)} %param.14) | copy-start | bytes 388
  249.6 3.3 collective-permute-start.2
  250.9 3.1 collective-permute-start.3
Sparse Core Ops, SparseCore 0:
  10.5 31.3 all-gather.1
  239.3 77.0 all-reduce.5
where the time goes:
time: 330 us; the launch traced here: 327 us
  blocking collectives  115 us (35%)
  waiting for transfers between devices  110 us (33%)
  other arithmetic  29.2 us (9%)
  local copies, waits for them, and re-layouts  20.6 us (6%)
  matrix products  19.2 us (6%)
  starting transfers between devices  17 us (5%)
  between operations  15.6 us (5%)
    all_to_all x1, blocking collectives, local(): lax.all_to_all(outgoing, 'tile', split_axis=1, concat_axis=1, tiled=True)  105 us
    unnamed x3, waiting for transfers between devices  62.4 us
    all_to_all x1, waiting for transfers between devices, local(): lax.all_to_all(lifted_tiles, 'tile', split_axis=1, concat_axis=1, tiled=T...  25.7 us
    scatter-add x2, other arithmetic, advance(): return totals.at[slots_here].add(per_block)  16.1 us
    all_gather x1, waiting for transfers between devices, local(): lax.all_gather(packed[None], 'grp', axis=0, tiled=True)  15.6 us
    all_gather x1, blocking collectives, local(): lax.all_gather(slot_flags[None], 'grp', axis=0, tiled=True)  9.65 us
    dot_general x2, matrix products, advance(): jnp.einsum('bfc,bpc->bfp', tile_values, one_hot, preferred_element_type=j...  8.68 us
    unnamed x16, local copies, waits for them, and re-layouts  8.53 us
  transfers between devices with their start and end apart: 8, of which 6 were waited for; matrix products, arithmetic and copies ran while one was open for 3% of the time, Pallas kernels for 0%

commit v1 on v0

--- a/solution.py
+++ b/solution.py
@@ -178,7 +178,12 @@
     outgoing = jnp.concatenate(
         [deposit.reshape(gas_groups, owners, slot_depth, nfield, tile_cells), zero_block], axis=0
     )
-    spread = lax.all_to_all(outgoing, "tile", split_axis=1, concat_axis=1, tiled=True)
+    spread = jnp.concatenate(
+        lax.all_to_all(
+            jnp.stack(jnp.split(outgoing, lax.axis_size("tile"), 1), axis=0), "tile", 0, 0
+        ),
+        axis=1,
+    )
     landed = lax.psum_scatter(spread, "grp", scatter_dimension=0, tiled=True)
     incoming = landed.reshape(owners * slot_depth, nfield * tile_cells)
     placed = jnp.dot(

time: 330 us -> 328 us (level)
    unnamed x16 -> x22, local copies, waits for them, and re-layouts: 8.53 us -> 5.68 us
where the time goes in v1:
time: 328 us; the launch traced here: 325 us
  blocking collectives  115 us (35%)
  waiting for transfers between devices  110 us (34%)
  other arithmetic  29.2 us (9%)
  matrix products  19.2 us (6%)
  local copies, waits for them, and re-layouts  18.6 us (6%)
  starting transfers between devices  17 us (5%)
  between operations  15.7 us (5%)
    all_to_all x1, blocking collectives, local(): lax.all_to_all(jnp.stack(jnp.split(outgoing, lax.axis_size('tile'), 1), a...  105 us
    unnamed x3, waiting for transfers between devices  62.4 us
    all_to_all x1, waiting for transfers between devices, local(): lax.all_to_all(lifted_tiles, 'tile', split_axis=1, concat_axis=1, tiled=T...  25.7 us
    scatter-add x2, other arithmetic, advance(): return totals.at[slots_here].add(per_block)  16.1 us
    all_gather x1, waiting for transfers between devices, local(): lax.all_gather(packed[None], 'grp', axis=0, tiled=True)  15.6 us
    all_gather x1, blocking collectives, local(): lax.all_gather(slot_flags[None], 'grp', axis=0, tiled=True)  9.65 us
    dot_general x2, matrix products, advance(): jnp.einsum('bfc,bpc->bfp', tile_values, one_hot, preferred_element_type=j...  8.68 us
    dot_general x2, matrix products, advance(): jnp.einsum('bfp,bpc->bfc', pieces, one_hot, preferred_element_type=jnp.fl...  8.16 us
  transfers between devices with their start and end apart: 8, of which 6 were waited for; matrix products, arithmetic and copies ran while one was open for 3% of the time, Pallas kernels for 0%

profile of v1, /device:TPU:0, one launch (start us, length us, event | category | flops | bytes accessed | tf_op | source)
XLA Modules:
  0.0 325.1 jit_solution(4745151491095784361)
XLA Ops:
  6.5 0.9 convert_reduce_fusion
  7.5 1.0 fusion.56
  8.5 0.1 copy.110
  8.7 1.7 convolution_convert_fusion
  10.4 0.7 select_reduce_fusion.1
  11.2 0.1 convert_element_type.87
  11.2 9.7 %all_gather.6 = s32[4,8,8]{2,1,0:T(8,128)S(1)} all-gather(s32[1,8,8]{2,1,0:T(8,128)S(1)} %convert_element_type.87), channel_id=1, replica_groups=mesh['grp'=4,'tile'=8] {'grp'}, dimensions={0}, use_global_device_ids=true | all-gather | bytes 1280 | tf_op jit(solution)/shard_map/all_gather | solution.py:108
  20.9 0.6 copy.107
  21.5 4.9 %all-to-all-start = ((s32[4,8,8]{2,0,1:T(4,128)}), s32[4,8,8]{2,0,1:T(4,128)S(1)}, u32[]{:S(2)}, u32[]{:S(2)}) async-start(s32[4,8,8]{2,0,1:T(4,128)} %copy.107), calls=%async_computation | async-start | bytes 32768 | tf_op jit(solution)/shard_map/all_to_all | solution.py:112
  26.4 15.6 %all-gather.2.cloned.1.call-done = bf16[4,8,8,5,512]{4,2,3,1,0:T(8,128)(2,1)} async-done(((bf16[1,8,8,5,512]{4,2,3,1,0:T(8,128)(2,1)}), bf16[4,8,8,5,512]{4,2,3,1,0:T(8,128)(2,1)}) %all-gather.2.cloned.1.call-update) | async-done | bytes 1310736 | tf_op jit(solution)/shard_map/all_gather | solution.py:107
  41.9 2.5 copy.111
  44.5 4.7 %all-to-all-start.1 = ((bf16[4,8,8,5,512]{4,2,3,0,1:T(8,128)(2,1)}), bf16[4,8,8,5,512]{4,2,3,0,1:T(8,128)(2,1)S(1)}, u32[]{:S(2)}, u32[]{:S(2)}) async-start(bf16[4,8,8,5,512]{4,2,3,0,1:T(8,128)(2,1)} %copy.111), calls=%async_computation.1 | async-start | bytes 2621440 | tf_op jit(solution)/shard_map/all_to_all | solution.py:111
  49.9 2.5 copy.142
  52.4 0.7 fusion.59
  54.4 0.1 broadcast_in_dim_reshape.7
  54.5 0.3 reduce-window.9
  54.9 0.1 slice_reduce_fusion
  55.1 0.4 broadcast_remainder_fusion
  55.5 0.2 select_reduce_fusion
  55.7 25.7 %all-to-all-done.1 = bf16[4,8,8,5,512]{4,2,3,0,1:T(8,128)(2,1)S(1)} async-done(((bf16[4,8,8,5,512]{4,2,3,0,1:T(8,128)(2,1)}), bf16[4,8,8,5,512]{4,2,3,0,1:T(8,128)(2,1)S(1)}, u32[]{:S(2)}, u32[]{:S(2)}) %all-to-all-start.1) | async-done | bytes 1310752 | tf_op jit(solution)/shard_map/all_to_all | solution.py:111
  81.4 0.1 slice.124
  81.5 0.1 copy.129
  81.6 0.6 copy.113
  82.2 2.1 broadcast_in_dim.54
  84.2 44.5 %while.14 = (s32[]{:T(128)}, f32[192,5,512]{2,1,0:T(8,128)}, s32[]{:T(128)}, s32[]{:T(128)}, s32[1024]{0:T(1024)S(1)}, /*index=5*/f32[1024,128]{1,0:T(8,128)}, f...) while((s32[]{:T(128)}, f32[192,5,512]{2,1,0:T(8,128)}, ...), condition=%wide.region_9.10_spmd.clone, body=%wide.region_6.9_spmd.clone.sunk | while | flops 178324864 | bytes 9770991 | solution.py:174
  84.2 0.1 compare_select_fusion.2
  84.3 0.6 gather_fusion
  84.9 0.8 constant_dynamic-slice_fusion.6
  85.7 4.3 %fusion.71 = f32[64,5,128]{2,1,0:T(8,128)S(1)} fusion(bf16[64,5,512]{2,1,0:T(8,128)(2,1)S(1)} %gather_fusion, s32[64,128]{1,0:T(8,128)S(1)} %constant_dynamic-slice_fusion.6), kind=kOutput, calls=%fused_computation.5.clone.1 | convolution fusion | flops 46137344 | bytes 524288 | tf_op jit(solution)/shard_map/while/body/bfc,bpc->bfp/dot_general | solution.py:152
  90.1 0.8 fusion.73
  91.0 1.0 multiply_reduce_fusion.2
  92.0 0.9 multiply_subtract_fusion.4
  92.9 1.0 multiply_subtract_fusion.5
  93.9 0.2 fusion.74
  94.1 4.1 %fusion.75 = f32[64,15,512]{2,1,0:T(8,128)S(1)} fusion(s32[64,128]{1,0:T(8,128)S(1)} %constant_dynamic-slice_fusion.6, bf16[64,5,128]{2,1,0:T(8,128)(2,1)S(1)} %get-tuple-element.392, bf16[64,5,128]{2,1,0:T(8,128)(2,1)S(1)} %get-tuple-element.393, bf16[64,5,128]{2,1,0:T(8,128)(2,1)S(1)} %get-tuple-element.394), kind=kOutput, calls=%fused_computation.4.clone.1 | convolution fusion | flops 130760704 | bytes 2244608 | tf_op jit(solution)/shard_map/while/body/bfp,bpc->bfc/dot_general | solution.py:168
  98.1 0.3 slice_add_fusion.7
  98.4 8.1 %scatter_fusion = f32[192,5,512]{2,1,0:T(8,128)} fusion(f32[192,5,512]{2,1,0:T(8,128)} %get-tuple-element.412, s32[64]{0:T(128)S(1)} %compare_select_fusion.2, f32[64,5,512]{2,1,0:T(8,128)S(1)} %slice_add_fusion.7), kind=kCustom, calls=%fused_computation.1.clone.clone.1 | custom fusion | flops 163840 | bytes 1966336 | tf_op jit(solution)/shard_map/while/body/scatter-add | solution.py:172
  106.5 0.6 gather_fusion
  107.1 0.8 constant_dynamic-slice_fusion.6
  107.9 4.3 %fusion.71 = f32[64,5,128]{2,1,0:T(8,128)S(1)} fusion(bf16[64,5,512]{2,1,0:T(8,128)(2,1)S(1)} %gather_fusion, s32[64,128]{1,0:T(8,128)S(1)} %constant_dynamic-slice_fusion.6), kind=kOutput, calls=%fused_computation.5.clone.1 | convolution fusion | flops 46137344 | bytes 524288 | tf_op jit(solution)/shard_map/while/body/bfc,bpc->bfp/dot_general | solution.py:152
  112.3 0.8 fusion.73
  113.2 1.0 multiply_reduce_fusion.2
  114.2 0.9 multiply_subtract_fusion.4
  115.1 1.0 multiply_subtract_fusion.5
  116.1 0.2 fusion.74
  116.3 4.1 %fusion.75 = f32[64,15,512]{2,1,0:T(8,128)S(1)} fusion(s32[64,128]{1,0:T(8,128)S(1)} %constant_dynamic-slice_fusion.6, bf16[64,5,128]{2,1,0:T(8,128)(2,1)S(1)} %get-tuple-element.392, bf16[64,5,128]{2,1,0:T(8,128)(2,1)S(1)} %get-tuple-element.393, bf16[64,5,128]{2,1,0:T(8,128)(2,1)S(1)} %get-tuple-element.394), kind=kOutput, calls=%fused_computation.4.clone.1 | convolution fusion | flops 130760704 | bytes 2244608 | tf_op jit(solution)/shard_map/while/body/bfp,bpc->bfc/dot_general | solution.py:168
  120.4 0.3 slice_add_fusion.7
  120.6 8.1 %scatter_fusion = f32[192,5,512]{2,1,0:T(8,128)} fusion(f32[192,5,512]{2,1,0:T(8,128)} %get-tuple-element.412, s32[64]{0:T(128)S(1)} %compare_select_fusion.2, f32[64,5,512]{2,1,0:T(8,128)S(1)} %slice_add_fusion.7), kind=kCustom, calls=%fused_computation.1.clone.clone.1 | custom fusion | flops 163840 | bytes 1966336 | tf_op jit(solution)/shard_map/while/body/scatter-add | solution.py:172
  128.7 3.0 copy.114
  132.0 105.4 %all_to_all.15 = f32[8,4,1,8,5,512]{5,3,1,4,2,0:T(8,128)} all-to-all(f32[8,4,1,8,5,512]{5,3,1,4,2,0:T(8,128)S(1)} %fusion.28), channel_id=1, replica_groups=mesh['grp'=4,'tile'=8] {'tile'}, dimensions={0} | all-to-all | bytes 5242880 | tf_op jit(solution)/shard_map/all_to_all | solution.py:182
  237.5 3.4 %collective-permute-start = (bf16[5,32,1,128]{3,1,2,0:T(8,128)(2,1)S(1)}, bf16[5,32,1,128]{3,1,2,0:T(8,128)(2,1)S(1)}, u32[]{:S(2)}, u32[]{:S(2)}) collective-permute-start(bf16[5,32,1,128]{3,1,2,0:T(8,128)(2,1)S(1)} %get-tuple-element.293), channel_id=1, source_target_pairs={{0,8},{8,16},{16,24},{1,9},{9,17},{17,25},{2,10},{10,18},{18,26},{... | collective-permute-start | bytes 122888 | tf_op jit(solution)/shard_map/ppermute | solution.py:14
  240.9 1.3 collective-permute-start.1
  242.2 1.0 collective-permute-done
  243.2 4.6 %collective-permute-done.1 = bf16[5,32,1,128]{3,1,2,0:T(8,128)(2,1)S(1)} collective-permute-done((bf16[5,32,1,128]{3,1,2,0:T(8,128)(2,1)S(1)}, bf16[5,32,1,128]{3,1,2,0:T(8,128)(2,1)S(1)}, u32[]{:S(2)}, u32[]{:S(2)}) %collective-permute-start.1) | collective-permute-done | bytes 40992 | tf_op jit(solution)/shard_map/ppermute | solution.py:17
  247.8 1.3 collective-permute-start.2
  249.1 1.3 collective-permute-start.3
  250.5 0.6 dynamic-slice
  251.1 1.1 collective-permute-done.3
  252.2 0.1 maximum_convert_fusion
  252.4 62.3 %all-reduce.6.cloned.1.call-done = f32[4,8,8,5,512]{4,2,0,3,1:T(8,128)} async-done(((f32[4,8,8,5,512]{4,2,0,3,1:T(8,128)}), f32[4,8,8,5,512]{4,2,0,3,1:T(8,128)}) %all-reduce.6.cloned.1.call-update) | async-done | bytes 2621456
  314.7 1.8 constant_dynamic-slice_fusion.3
  316.5 0.2 dot_general.26
  316.7 0.6 fusion.18
  317.3 0.9 copy.123
  (46 shorter events, 0.9 us)
Async XLA Ops:
  6.5 35.4 %all-gather.2.cloned.1.call-start = ((), (), s32[]{:S(2)}) async-start(), calls=%async_computation.3 | async-start | bytes 1638400 | tf_op jit(solution)/shard_map/all_gather | solution.py:107
  21.5 23.0 %all-to-all-start = ((s32[4,8,8]{2,0,1:T(4,128)}), s32[4,8,8]{2,0,1:T(4,128)S(1)}, u32[]{:S(2)}, u32[]{:S(2)}) async-start(s32[4,8,8]{2,0,1:T(4,128)} %copy.107), calls=%async_computation | async-start | bytes 32768 | tf_op jit(solution)/shard_map/all_to_all | solution.py:112
  26.4 23.5 %copy-start = (f32[1,1024,3,128]{3,1,2,0:T(8,128)S(1)}, f32[1,1024,3,128]{3,1,2,0:T(8,128)}, u32[]{:S(2)}) copy-start(f32[1,1024,3,128]{3,1,2,0:T(8,128)} %param.17) | copy-start | bytes 4718596
  44.5 10.6 %copy-start.2 = (s32[1,1024]{1,0:T(1,128)S(1)}, s32[1,1024]{1,0:T(1,128)}, u32[]{:S(2)}) copy-start(s32[1,1024]{1,0:T(1,128)} %param.16) | copy-start | bytes 12292
  44.5 36.9 %all-to-all-start.1 = ((bf16[4,8,8,5,512]{4,2,3,0,1:T(8,128)(2,1)}), bf16[4,8,8,5,512]{4,2,3,0,1:T(8,128)(2,1)S(1)}, u32[]{:S(2)}, u32[]{:S(2)}) async-start(bf16[4,8,8,5,512]{4,2,3,0,1:T(8,128)(2,1)} %copy.111), calls=%async_computation.1 | async-start | bytes 2621440 | tf_op jit(solution)/shard_map/all_to_all | solution.py:111
  49.2 265.5 %all-reduce.6.cloned.1.call-start = ((), (), s32[]{:S(2)}) async-start(), calls=%async_computation.4 | async-start | bytes 5242880
  237.4 13.0 %copy-start.1 = (f32[32,4,128]{2,1,0:T(4,128)S(1)}, f32[32,4,128]{2,1,0:T(4,128)}, u32[]{:S(2)}) copy-start(f32[32,4,128]{2,1,0:T(4,128)} %param.13) | copy-start | bytes 196612
  237.4 13.1 %copy-start.4 = (u32[32]{0:T(128)S(1)}, u32[32]{0:T(128)}, u32[]{:S(2)}) copy-start(u32[32]{0:T(128)} %constant.197) | copy-start | bytes 388
  237.5 79.3 %copy-start.3 = (s32[1,32,1]{1,2,0:T(1,128)S(1)}, s32[1,32,1]{1,2,0:T(1,128)}, u32[]{:S(2)}) copy-start(s32[1,32,1]{1,2,0:T(1,128)} %param.14) | copy-start | bytes 388
  237.5 5.8 %collective-permute-start = (bf16[5,32,1,128]{3,1,2,0:T(8,128)(2,1)S(1)}, bf16[5,32,1,128]{3,1,2,0:T(8,128)(2,1)S(1)}, u32[]{:S(2)}, u32[]{:S(2)}) collective-permute-start(bf16[5,32,1,128]{3,1,2,0:T(8,128)(2,1)S(1)} %get-tuple-element.293), channel_id=1, source_target_pairs={{0,8},{8,16},{16,24},{1,9},{9,17},{17,25},{2,10},{10,18},{18,26},{... | collective-permute-start | bytes 122888 | tf_op jit(solution)/shard_map/ppermute | solution.py:14
  240.9 6.9 %collective-permute-start.1 = (bf16[5,32,1,128]{3,1,2,0:T(8,128)(2,1)S(1)}, bf16[5,32,1,128]{3,1,2,0:T(8,128)(2,1)S(1)}, u32[]{:S(2)}, u32[]{:S(2)}) collective-permute-start(bf16[5,32,1,128]{3,1,2,0:T(8,128)(2,1)S(1)} %get-tuple-element.294), channel_id=1, source_target_pairs={{8,0},{16,8},{24,16},{9,1},{17,9},{25,17},{10,2},{18,10},{26,18},{... | collective-permute-start | bytes 122888 | tf_op jit(solution)/shard_map/ppermute | solution.py:17
  247.8 3.3 %collective-permute-start.2 = (bf16[5,1,6,128]{3,1,2,0:T(2,128)(2,1)S(1)}, bf16[5,1,6,128]{3,1,2,0:T(2,128)(2,1)S(1)}, u32[]{:S(2)}, u32[]{:S(2)}) collective-permute-start(bf16[5,1,6,128]{3,1,2,0:T(2,128)(2,1)S(1)} %get-tuple-element.291), channel_id=1, source_target_pairs={{0,1},{1,2},{2,3},{3,4},{4,5},{5,6},{6,7},{8,9},{9,10},{10,11},{11... | collective-permute-start | bytes 23048 | tf_op jit(solution)/shard_map/ppermute | solution.py:14
  249.1 3.1 collective-permute-start.3
Sparse Core Ops, SparseCore 0:
  10.5 31.3 all-gather.1
  237.6 77.0 all-reduce.5
